TPU v7x, 256 devices: a whole 4x4x8 slice. The times are simulated.
256 devices in a mesh: tgt: 64 (over x, z, core), sec: 4 (over y).
Axes of the slice: x: 4, y: 4, z: 8, core: 2. Of those that a mesh axis runs over, the one named last changes fastest.
Arguments:
- queries: bfloat16 [16384, 4096], P('tgt', 'sec'), may hold values from -210 to 210
- key_values: bfloat16 [2, 16384, 4096], P(None, 'tgt', 'sec'), may hold values from -6.06 to 6.06
- grad_out: bfloat16 [16384, 4096], P('tgt', 'sec'), may hold values from -192 to 192
- block_ids: int32 [128, 4], P('tgt'), may hold values from 0 to 127, as said below
- block_count: int32 [128], P('tgt'), may hold values from 1 to 4, as said below
- kv_weight: bfloat16 [2, 4096, 4096], P(None, 'tgt', 'sec'), may hold values from -0.0625 to 0.0625
Outputs:
- grad_queries: bfloat16 [16384, 4096], P('tgt', 'sec')
- grad_memory: bfloat16 [16384, 4096], P('tgt', 'sec')
Inputs may be any that keep to these rules, and one draw needn't show every extreme that they name: `block_ids`: target block i, which lies in the rows of index t = i // 2 of tgt, lists only source blocks in the rows of indices t - 1, t and t + 1; its first entry is block i itself; its live entries are distinct; entries past its count repeat block i. `block_count`: every eighth block, starting at block 3, has all slots live.
All inputs are finite; a program needn't handle non-finite values.
Results may differ from a plain program's by a relative error of at most 0.013.
Values may be sent and summed in bfloat16 or wider, within the bound.
A program may use at most 128 MiB of HBM per device.

v0:
```python
import jax
import jax.numpy as jnp
from jax import lax
from jax.sharding import PartitionSpec as P

HEAD_DIM = 64
BLOCK = 128
SLOTS = 4


def from_behind(block, axis, distance):
    devices = range(lax.axis_size(axis))
    route = [(i - distance, i) for i in devices if i - distance in devices]
    return lax.ppermute(block, axis, route)


def with_halo(block, sides, width):
    for axis, dim in sides:
        count = lax.axis_size(axis)
        forward = [(i, i + 1) for i in range(count - 1)]
        backward = [(target, source) for source, target in forward]
        low = lax.ppermute(
            lax.slice_in_dim(block, block.shape[dim] - width, None, axis=dim), axis, forward
        )
        high = lax.ppermute(lax.slice_in_dim(block, 0, width, axis=dim), axis, backward)
        block = jnp.concatenate([low, block, high], axis=dim)
    return block


def send_back(part_grads, offset):
    return from_behind(part_grads.astype(jnp.bfloat16), "tgt", offset).astype(part_grads.dtype)


def per_device(queries, key_values, grad_out, block_ids, block_count, kv_weight):
    rows_here = queries.shape[0]
    width_here = queries.shape[1]
    heads_here = width_here // HEAD_DIM
    blocks_here = rows_here // BLOCK
    device_pos = lax.axis_index("tgt")
    extended = with_halo(key_values, (("tgt", 1),), rows_here)
    local_ids = block_ids - (device_pos - 1) * blocks_here
    ext_blocks = extended.reshape(2, 3 * blocks_here, BLOCK, width_here)
    ext_range = jnp.arange(3 * blocks_here)

    def block_step(carry, inputs):
        query_block, upstream_block, listed, count = inputs
        picked = ext_blocks[:, listed]
        key_rows = picked[0].reshape(SLOTS * BLOCK, heads_here, HEAD_DIM)
        value_rows = picked[1].reshape(SLOTS * BLOCK, heads_here, HEAD_DIM)
        query_rows = query_block.reshape(BLOCK, heads_here, HEAD_DIM)
        upstream = upstream_block.reshape(BLOCK, heads_here, HEAD_DIM)
        slot_live = jnp.arange(SLOTS) < count
        key_live = jnp.repeat(slot_live, BLOCK)
        scores = 0.125 * jnp.einsum(
            "qhd,khd->hqk", query_rows, key_rows, preferred_element_type=jnp.float32
        )
        scores = jnp.where(key_live[None, None, :], scores, -jnp.inf)
        row_max = jnp.max(scores, axis=-1, keepdims=True)
        expo = jnp.exp(scores - row_max)
        probs = expo / jnp.sum(expo, axis=-1, keepdims=True)
        probs_half = probs.astype(jnp.bfloat16)
        attended = jnp.einsum(
            "hqk,khd->qhd", probs_half, value_rows, preferred_element_type=jnp.float32
        )
        delta = jnp.sum(upstream.astype(jnp.float32) * attended, axis=-1)
        grad_probs = jnp.einsum(
            "qhd,khd->hqk", upstream, value_rows, preferred_element_type=jnp.float32
        )
        grad_scores = probs * (grad_probs - jnp.transpose(delta)[:, :, None])
        grad_half = grad_scores.astype(jnp.bfloat16)
        grad_query = 0.125 * jnp.einsum(
            "hqk,khd->qhd", grad_half, key_rows, preferred_element_type=jnp.float32
        )
        grad_key = 0.125 * jnp.einsum(
            "hqk,qhd->khd", grad_half, query_rows, preferred_element_type=jnp.float32
        )
        grad_value = jnp.einsum(
            "hqk,qhd->khd", probs_half, upstream, preferred_element_type=jnp.float32
        )
        pair_grads = jnp.stack([grad_key, grad_value]).reshape(2, SLOTS, BLOCK, width_here)
        targets = ((listed[:, None] == ext_range[None, :]) & slot_live[:, None]).astype(jnp.float32)
        carry = carry + jnp.einsum(
            "sj,csrx->cjrx", targets, pair_grads, precision=lax.Precision.HIGHEST
        )
        return (carry, grad_query.reshape(BLOCK, width_here).astype(jnp.bfloat16))

    start = jnp.zeros((2, 3 * blocks_here, BLOCK, width_here), jnp.float32)
    inputs = (
        queries.reshape(blocks_here, BLOCK, width_here),
        grad_out.reshape(blocks_here, BLOCK, width_here),
        local_ids,
        block_count,
    )
    spread_blocks, query_blocks = lax.scan(block_step, start, inputs)
    spread = spread_blocks.reshape(2, 3 * rows_here, width_here)
    own_grads = spread[:, rows_here : 2 * rows_here]
    own_grads = (
        own_grads + send_back(spread[:, :rows_here], -1) + send_back(spread[:, 2 * rows_here :], 1)
    )
    grads_half = own_grads.astype(jnp.bfloat16)
    partial_memory = jnp.einsum(
        "crx,cnx->rn",
        grads_half,
        lax.all_gather(kv_weight, "tgt", axis=1, tiled=True),
        preferred_element_type=jnp.float32,
    )
    total_memory = lax.psum(partial_memory.astype(jnp.bfloat16), "sec").astype(jnp.float32)
    columns = total_memory.shape[1] // lax.axis_size("sec")
    grad_memory = lax.dynamic_slice_in_dim(
        total_memory, lax.axis_index("sec") * columns, columns, 1
    ).astype(jnp.bfloat16)
    grad_queries = query_blocks.reshape(rows_here, width_here)
    return (grad_queries, grad_memory)


def solution(mesh):
    return jax.shard_map(
        per_device,
        mesh=mesh,
        in_specs=(
            P("tgt", "sec"),
            P(None, "tgt", "sec"),
            P("tgt", "sec"),
            P("tgt", None),
            P("tgt"),
            P(None, "tgt", "sec"),
        ),
        out_specs=(P("tgt", "sec"), P("tgt", "sec")),
        check_vma=False,
    )
```

profile of v0, /device:TPU:1, one launch (start us, length us, event | category | flops | bytes accessed | tf_op | source)
XLA Modules:
  0.0 269.9 jit_solution(8418963483960269523)
XLA Ops:
  7.9 4.9 %collective-permute-start = (bf16[2,256,1024]{2,1,0:T(8,128)(2,1)}, bf16[2,256,1024]{2,1,0:T(8,128)(2,1)S(1)}, u32[]{:S(2)}, u32[]{:S(2)}) collective-permute-start(bf16[2,256,1024]{2,1,0:T(8,128)(2,1)} %param.9), channel_id=1, source_target_pairs={{0,4},{4,8},{8,12},{12,16},{16,20},{20,24},{24,28},{28,32},{32,36}... | collective-permute-start | bytes 3145736 | tf_op jit(solution)/shard_map/ppermute | solution.py:22
  15.5 9.4 %collective-permute-done = bf16[2,256,1024]{2,1,0:T(8,128)(2,1)S(1)} collective-permute-done((bf16[2,256,1024]{2,1,0:T(8,128)(2,1)}, bf16[2,256,1024]{2,1,0:T(8,128)(2,1)S(1)}, u32[]{:S(2)}, u32[]{:S(2)}) %collective-permute-start) | collective-permute-done | bytes 1048608 | tf_op jit(solution)/shard_map/ppermute | solution.py:22
  24.9 4.3 %collective-permute-done.1 = bf16[2,256,1024]{2,1,0:T(8,128)(2,1)S(1)} collective-permute-done((bf16[2,256,1024]{2,1,0:T(8,128)(2,1)}, bf16[2,256,1024]{2,1,0:T(8,128)(2,1)S(1)}, u32[]{:S(2)}, u32[]{:S(2)}) %collective-permute-start.1) | collective-permute-done | bytes 1048608 | tf_op jit(solution)/shard_map/ppermute | solution.py:25
  29.2 2.8 %pad_maximum_fusion = bf16[2,768,1024]{2,1,0:T(8,128)(2,1)} fusion(bf16[2,256,1024]{2,1,0:T(8,128)(2,1)S(1)} %collective-permute-done.1, bf16[2,256,1024]{2,1,0:T(8,128)(2,1)} %param.9, bf16[2,256,1024]{2,1,0:T(8,128)(2,1)S(1)} %collective-permute-done), kind=kLoop, calls=%fused_computation.45 | loop fusion | flops 9437184 | bytes 6291456 | tf_op jit(solution)/shard_map/concatenate | solution.py:26
  32.0 116.6 %while.13 = (s32[]{:T(128)}, f32[2,6,128,1024]{3,1,2,0:T(8,128)}, bf16[2,128,1024]{2,1,0:T(8,128)(2,1)}, bf16[2,128,1024]{2,1,0:T(8,128)(2,1)}, s32[2]{0:T(128)S...) while((s32[]{:T(128)}, f32[2,6,128,1024]{3,1,2,0:T(8,128)}, ...), condition=%wide.region_4.5_spmd.clone, body=%wide.region_0.4_spmd.clone.sunk | while | flops 896663104 | bytes 128497184 | solution.py:94
  39.5 3.4 %fusion.88 = (f32[16,128]{1,0:T(8,128)S(1)}, f32[16,128,512]{2,1,0:T(8,128)}) fusion(pred[512]{0:T(512)(128)(4,1)S(1)} %broadcast_bitcast_fusion.2, bf16[128,16,64]{0,2,1:T(8,128)(2,1)S(1)} %bitcast.125, bf16[512,16,64]{0,2,1:T(8,128)(2,1)S(1)} %squeeze.23), kind=kOutput, calls=%fused_computation.53.clone.1 | convolution fusion | flops 138412544 | bytes 5513728 | tf_op jit(solution)/shard_map/while/body/eval_jaxpr/sub | solution.py:59
  53.4 2.8 %multiply_convert_fusion.2 = bf16[16,128,512]{2,1,0:T(8,128)(2,1)S(1)} fusion(bf16[128,16,64]{0,2,1:T(8,128)(2,1)S(1)} %bitcast.123, bf16[512,16,64]{0,2,1:T(8,128)(2,1)S(1)} %copy-done.3, f32[16,128]{1,0:T(8,128)S(1)} %bitcast.131, f32[16,128,512]{2,1,0:T(8,128)} %get-tuple-element.171, f32[16,128]{1,0:T(8,128)S(1)} %get-tuple-element.172), kind=kOutput, calls=%fused_computation.8.clone.1 | convolution fusion | flops 138412032 | bytes 7618560 | tf_op jit(solution)/shard_map/while/body/eval_jaxpr/qhd,khd->hqk/dot_general | solution.py:66
  59.4 2.9 %stack.15 = f32[1,4,128,1024]{2,1,3,0:T(4,128)} reshape(f32[512,16,64]{0,2,1:T(8,128)} %multiply_bitcast_fusion.2) | data formatting | bytes 4194304 | tf_op jit(solution)/shard_map/while/body/eval_jaxpr/stack | solution.py:80
  62.3 3.9 %copy.38 = f32[1,4,128,1024]{3,1,2,0:T(4,128)} copy(f32[1,4,128,1024]{2,1,3,0:T(4,128)} %stack.15) | data formatting | bytes 4194304 | tf_op jit(solution)/shard_map/while/body/eval_jaxpr/stack | solution.py:80
  67.9 2.9 %stack.14 = f32[1,4,128,1024]{2,1,3,0:T(4,128)} reshape(f32[512,16,64]{0,2,1:T(8,128)} %convolution_bitcast_fusion.4) | data formatting | bytes 4194304 | tf_op jit(solution)/shard_map/while/body/eval_jaxpr/stack | solution.py:80
  70.8 4.1 %copy.36 = f32[1,4,128,1024]{3,1,2,0:T(4,128)} copy(f32[1,4,128,1024]{2,1,3,0:T(4,128)} %stack.14) | data formatting | bytes 4194304 | tf_op jit(solution)/shard_map/while/body/eval_jaxpr/stack | solution.py:80
  74.9 12.2 %bitcast_add_fusion.2 = f32[2,6,128,1024]{3,1,2,0:T(8,128)} fusion(f32[2,6,128,1024]{3,1,2,0:T(8,128)} %get-tuple-element.185, pred[]{:T(512)S(6)} %compare.3, f32[1,4,128,1024]{3,1,2,0:T(4,128)} %copy.36, f32[1,4,128,1024]{3,1,2,0:T(4,128)S(1)} %copy-done, s32[4]{0:T(128)S(1)} %fusion.91, pred[4]{0:T(512)(128)(4,1)S(1)} %iota_compare_fusion.3), kind=kOutput, calls=%fused_computation.3.clone.1 | convolution fusion | flops 79691824 | bytes 16777236 | tf_op jit(solution)/shard_map/while/body/eval_jaxpr/sj,csrx->cjrx/dot_general | solution.py:82
  96.6 3.4 %fusion.88 = (f32[16,128]{1,0:T(8,128)S(1)}, f32[16,128,512]{2,1,0:T(8,128)}) fusion(pred[512]{0:T(512)(128)(4,1)S(1)} %broadcast_bitcast_fusion.2, bf16[128,16,64]{0,2,1:T(8,128)(2,1)S(1)} %bitcast.125, bf16[512,16,64]{0,2,1:T(8,128)(2,1)S(1)} %squeeze.23), kind=kOutput, calls=%fused_computation.53.clone.1 | convolution fusion | flops 138412544 | bytes 5513728 | tf_op jit(solution)/shard_map/while/body/eval_jaxpr/sub | solution.py:59
  110.6 2.9 %multiply_convert_fusion.2 = bf16[16,128,512]{2,1,0:T(8,128)(2,1)S(1)} fusion(bf16[128,16,64]{0,2,1:T(8,128)(2,1)S(1)} %bitcast.123, bf16[512,16,64]{0,2,1:T(8,128)(2,1)S(1)} %copy-done.3, f32[16,128]{1,0:T(8,128)S(1)} %bitcast.131, f32[16,128,512]{2,1,0:T(8,128)} %get-tuple-element.171, f32[16,128]{1,0:T(8,128)S(1)} %get-tuple-element.172), kind=kOutput, calls=%fused_computation.8.clone.1 | convolution fusion | flops 138412032 | bytes 7618560 | tf_op jit(solution)/shard_map/while/body/eval_jaxpr/qhd,khd->hqk/dot_general | solution.py:66
  116.7 2.9 %stack.15 = f32[1,4,128,1024]{2,1,3,0:T(4,128)} reshape(f32[512,16,64]{0,2,1:T(8,128)} %multiply_bitcast_fusion.2) | data formatting | bytes 4194304 | tf_op jit(solution)/shard_map/while/body/eval_jaxpr/stack | solution.py:80
  119.6 3.9 %copy.38 = f32[1,4,128,1024]{3,1,2,0:T(4,128)} copy(f32[1,4,128,1024]{2,1,3,0:T(4,128)} %stack.15) | data formatting | bytes 4194304 | tf_op jit(solution)/shard_map/while/body/eval_jaxpr/stack | solution.py:80
  125.3 2.9 %stack.14 = f32[1,4,128,1024]{2,1,3,0:T(4,128)} reshape(f32[512,16,64]{0,2,1:T(8,128)} %convolution_bitcast_fusion.4) | data formatting | bytes 4194304 | tf_op jit(solution)/shard_map/while/body/eval_jaxpr/stack | solution.py:80
  128.2 4.1 %copy.36 = f32[1,4,128,1024]{3,1,2,0:T(4,128)} copy(f32[1,4,128,1024]{2,1,3,0:T(4,128)} %stack.14) | data formatting | bytes 4194304 | tf_op jit(solution)/shard_map/while/body/eval_jaxpr/stack | solution.py:80
  132.3 14.5 %bitcast_add_fusion.2 = f32[2,6,128,1024]{3,1,2,0:T(8,128)} fusion(f32[2,6,128,1024]{3,1,2,0:T(8,128)} %get-tuple-element.185, pred[]{:T(512)S(6)} %compare.3, f32[1,4,128,1024]{3,1,2,0:T(4,128)} %copy.36, f32[1,4,128,1024]{3,1,2,0:T(4,128)S(1)} %copy-done, s32[4]{0:T(128)S(1)} %fusion.91, pred[4]{0:T(512)(128)(4,1)S(1)} %iota_compare_fusion.3), kind=kOutput, calls=%fused_computation.3.clone.1 | convolution fusion | flops 79691824 | bytes 16777236 | tf_op jit(solution)/shard_map/while/body/eval_jaxpr/sj,csrx->cjrx/dot_general | solution.py:82
  148.6 7.0 %copy.20 = f32[2,6,128,1024]{3,2,1,0:T(8,128)S(1)} copy(f32[2,6,128,1024]{3,1,2,0:T(8,128)} %get-tuple-element.51) | data formatting | bytes 12582912 | tf_op jit(solution)/shard_map/while | solution.py:94
  160.4 3.6 %collective-permute-start.3 = (bf16[2,256,1024]{2,1,0:T(8,128)(2,1)S(1)}, bf16[2,256,1024]{2,1,0:T(8,128)(2,1)S(1)}, u32[]{:S(2)}, u32[]{:S(2)}) collective-permute-start(bf16[2,256,1024]{2,1,0:T(8,128)(2,1)S(1)} %get-tuple-element.112), channel_id=1, source_target_pairs={{0,4},{4,8},{8,12},{12,16},{16,20},{20,24},{24,28},{28,32},{32,36}... | collective-permute-start | bytes 3145736 | tf_op jit(solution)/shard_map/ppermute | solution.py:14
  164.0 10.5 %collective-permute-done.2 = bf16[2,256,1024]{2,1,0:T(8,128)(2,1)S(1)} collective-permute-done((bf16[2,256,1024]{2,1,0:T(8,128)(2,1)S(1)}, bf16[2,256,1024]{2,1,0:T(8,128)(2,1)S(1)}, u32[]{:S(2)}, u32[]{:S(2)}) %collective-permute-start.2) | collective-permute-done | bytes 1048608 | tf_op jit(solution)/shard_map/ppermute | solution.py:14
  175.8 12.3 %fusion.29 = bf16[256,4096]{1,0:T(8,128)(2,1)} fusion(bf16[2,4096,1024]{2,1,0:T(8,128)(2,1)} %all-gather.2.cloned.1.call-done, f32[2,768,1024]{2,1,0:T(8,128)} %bitcast.128, bf16[2,256,1024]{2,1,0:T(8,128)(2,1)S(1)} %collective-permute-done.3, bf16[2,256,1024]{2,1,0:T(8,128)(2,1)S(1)} %collective-permute-done.2), kind=kOutput, calls=%fused_computation.44 | convolution fusion | flops 4298637312 | bytes 23068672 | tf_op jit(solution)/shard_map/crx,cnx->rn/dot_general | solution.py:101
  188.1 73.1 %all-reduce.2.cloned.1.call-done = bf16[256,4096]{1,0:T(8,128)(2,1)} async-done(((bf16[256,4096]{1,0:T(8,128)(2,1)}), bf16[256,4096]{1,0:T(8,128)(2,1)}) %all-reduce.2.cloned.1.call-update) | async-done | bytes 2097168 | tf_op jit(solution)/shard_map/psum | solution.py:107
  (102 shorter events, 60.6 us)
Async XLA Ops:
  7.2 168.6 %all-gather.2.cloned.1.call-start = ((), (), s32[]{:S(2)}) async-start(), calls=%async_computation | async-start | bytes 17039360 | tf_op jit(solution)/shard_map/all_gather | solution.py:104
  7.9 253.3 %all-reduce.2.cloned.1.call-start = ((), (), s32[]{:S(2)}) async-start(), calls=%async_computation.1 | async-start | bytes 4194304 | tf_op jit(solution)/shard_map/psum | solution.py:107
  7.9 17.0 %collective-permute-start = (bf16[2,256,1024]{2,1,0:T(8,128)(2,1)}, bf16[2,256,1024]{2,1,0:T(8,128)(2,1)S(1)}, u32[]{:S(2)}, u32[]{:S(2)}) collective-permute-start(bf16[2,256,1024]{2,1,0:T(8,128)(2,1)} %param.9), channel_id=1, source_target_pairs={{0,4},{4,8},{8,12},{12,16},{16,20},{20,24},{24,28},{28,32},{32,36}... | collective-permute-start | bytes 3145736 | tf_op jit(solution)/shard_map/ppermute | solution.py:22
  12.9 16.3 %collective-permute-start.1 = (bf16[2,256,1024]{2,1,0:T(8,128)(2,1)}, bf16[2,256,1024]{2,1,0:T(8,128)(2,1)S(1)}, u32[]{:S(2)}, u32[]{:S(2)}) collective-permute-start(bf16[2,256,1024]{2,1,0:T(8,128)(2,1)} %param.9), channel_id=1, source_target_pairs={{4,0},{8,4},{12,8},{16,12},{20,16},{24,20},{28,24},{32,28},{36,32}... | collective-permute-start | bytes 3145736 | tf_op jit(solution)/shard_map/ppermute | solution.py:25
  15.5 16.5 %copy-start.11 = (s32[2]{0:T(128)S(1)}, s32[2]{0:T(128)}, u32[]{:S(2)}) copy-start(s32[2]{0:T(128)} %param.12) | copy-start | bytes 28
  35.9 1.2 copy-start.7
  35.9 1.2 copy-start.8
  38.1 4.8 %copy-start.4 = (bf16[1,128,1024]{1,2,0:T(8,128)(2,1)}, bf16[1,128,1024]{1,2,0:T(8,128)(2,1)S(1)}, u32[]{:S(2)}) copy-start(bf16[1,128,1024]{1,2,0:T(8,128)(2,1)S(1)} %copy.34) | copy-start | bytes 786436 | tf_op jit(solution)/shard_map/while
  51.2 2.2 copy-start.3
  53.4 4.2 %copy-start.5 = (bf16[1,128,1024]{1,2,0:T(8,128)(2,1)S(1)}, bf16[1,128,1024]{1,2,0:T(8,128)(2,1)}, u32[]{:S(2)}) copy-start(bf16[1,128,1024]{1,2,0:T(8,128)(2,1)} %copy-done.4) | copy-start | bytes 786436 | tf_op jit(solution)/shard_map/while
  56.2 1.4 copy-start.1
  70.8 4.1 %copy-start = (f32[1,4,128,1024]{3,1,2,0:T(4,128)S(1)}, f32[1,4,128,1024]{3,1,2,0:T(4,128)}, u32[]{:S(2)}) copy-start(f32[1,4,128,1024]{3,1,2,0:T(4,128)} %copy.38) | copy-start | bytes 6291460 | tf_op jit(solution)/shard_map/while
  74.9 12.2 %copy-start.2 = (bf16[16,128,512]{2,1,0:T(8,128)(2,1)S(1)}, bf16[16,128,512]{2,1,0:T(8,128)(2,1)}, u32[]{:S(2)}) copy-start(bf16[16,128,512]{2,1,0:T(8,128)(2,1)} %copy-done.1) | copy-start | bytes 6291460 | tf_op jit(solution)/shard_map/while
  93.1 1.2 copy-start.7
  93.1 1.2 copy-start.8
  95.2 4.8 %copy-start.4 = (bf16[1,128,1024]{1,2,0:T(8,128)(2,1)}, bf16[1,128,1024]{1,2,0:T(8,128)(2,1)S(1)}, u32[]{:S(2)}) copy-start(bf16[1,128,1024]{1,2,0:T(8,128)(2,1)S(1)} %copy.34) | copy-start | bytes 786436 | tf_op jit(solution)/shard_map/while
  108.4 2.2 copy-start.3
  110.6 4.3 %copy-start.5 = (bf16[1,128,1024]{1,2,0:T(8,128)(2,1)S(1)}, bf16[1,128,1024]{1,2,0:T(8,128)(2,1)}, u32[]{:S(2)}) copy-start(bf16[1,128,1024]{1,2,0:T(8,128)(2,1)} %copy-done.4) | copy-start | bytes 786436 | tf_op jit(solution)/shard_map/while
  113.6 1.4 copy-start.1
  128.2 4.1 %copy-start = (f32[1,4,128,1024]{3,1,2,0:T(4,128)S(1)}, f32[1,4,128,1024]{3,1,2,0:T(4,128)}, u32[]{:S(2)}) copy-start(f32[1,4,128,1024]{3,1,2,0:T(4,128)} %copy.38) | copy-start | bytes 6291460 | tf_op jit(solution)/shard_map/while
  132.2 14.5 %copy-start.2 = (bf16[16,128,512]{2,1,0:T(8,128)(2,1)S(1)}, bf16[16,128,512]{2,1,0:T(8,128)(2,1)}, u32[]{:S(2)}) copy-start(bf16[16,128,512]{2,1,0:T(8,128)(2,1)} %copy-done.1) | copy-start | bytes 6291460 | tf_op jit(solution)/shard_map/while
  155.6 2.7 copy-start.6
  158.5 16.1 %collective-permute-start.2 = (bf16[2,256,1024]{2,1,0:T(8,128)(2,1)S(1)}, bf16[2,256,1024]{2,1,0:T(8,128)(2,1)S(1)}, u32[]{:S(2)}, u32[]{:S(2)}) collective-permute-start(bf16[2,256,1024]{2,1,0:T(8,128)(2,1)S(1)} %get-tuple-element.111), channel_id=1, source_target_pairs={{4,0},{8,4},{12,8},{16,12},{20,16},{24,20},{28,24},{32,28},{36,32}... | collective-permute-start | bytes 3145736 | tf_op jit(solution)/shard_map/ppermute | solution.py:14
  160.4 15.4 %collective-permute-start.3 = (bf16[2,256,1024]{2,1,0:T(8,128)(2,1)S(1)}, bf16[2,256,1024]{2,1,0:T(8,128)(2,1)S(1)}, u32[]{:S(2)}, u32[]{:S(2)}) collective-permute-start(bf16[2,256,1024]{2,1,0:T(8,128)(2,1)S(1)} %get-tuple-element.112), channel_id=1, source_target_pairs={{0,4},{4,8},{8,12},{12,16},{16,20},{20,24},{24,28},{28,32},{32,36}... | collective-permute-start | bytes 3145736 | tf_op jit(solution)/shard_map/ppermute | solution.py:14
  (4 other events, 3.8 us)
Sparse Core Ops, SparseCore 0:
  10.8 104.2 all-gather.1
  188.2 72.9 all-reduce.1
where the time goes:
time: 271 us; the launch traced here: 270 us
  waiting for transfers between devices  99.2 us (37%)
  local copies, waits for them, and re-layouts  67 us (25%)
  matrix products  64.3 us (24%)
  between operations  14.1 us (5%)
  starting transfers between devices  12.5 us (5%)
  other arithmetic  12.4 us (5%)
    psum x1, waiting for transfers between devices, per_device(): lax.psum(partial_memory.astype(jnp.bfloat16), 'sec').astype(jnp.float32)  73.1 us
    another operation x8, local copies, waits for them, and re-layouts, block_step(): jnp.stack([grad_key, grad_value]).reshape(2, SLOTS, BLOCK, width_here)  27.6 us
    dot_general x2, matrix products, block_step(): jnp.einsum('sj,csrx->cjrx', targets, pair_grads, precision=lax.Precision....  26.7 us
    dot_general x1, matrix products, per_device(): jnp.einsum('crx,cnx->rn', grads_half, lax.all_gather(kv_weight, 'tgt', ax...  12.3 us
    ppermute x2, waiting for transfers between devices, from_behind(): return lax.ppermute(block, axis, route)  11.7 us
    ppermute x1, waiting for transfers between devices, with_halo(): lax.ppermute(lax.slice_in_dim(block, block.shape[dim] - width, None, axis...  9.39 us
    slice x4, local copies, waits for them, and re-layouts, block_step(): value_rows = picked[1].reshape(SLOTS * BLOCK, heads_here, HEAD_DIM)  7.31 us
    while x1, local copies, waits for them, and re-layouts, per_device(): spread_blocks, query_blocks = lax.scan(block_step, start, inputs)  7.02 us
  transfers between devices with their start and end apart: 6, of which 5 were waited for; matrix products, arithmetic and copies ran while one was open for 45% of the time, Pallas kernels for 0%

commit v1 on v0

v1 whole, which is shorter than its diff:
```python
import functools

import jax
import jax.numpy as jnp
from jax import lax
from jax.experimental import pallas as pl
from jax.experimental.pallas import tpu as pltpu
from jax.sharding import PartitionSpec as P

MESH = pl.DeviceIdType.MESH
BLOCK = 128
SLOTS = 4
EXT = 6
PAIRS = 8
NX, NZ, NY = 4, 8, 4
LEAD = 48
F32 = jnp.float32
BF16 = jnp.bfloat16


def nt(a, b):
    return lax.dot_general(a, b, (((1,), (1,)), ((), ())), preferred_element_type=F32)


def nn(a, b):
    return lax.dot_general(a, b, (((1,), (0,)), ((), ())), preferred_element_type=F32)


def tn(a, b):
    return lax.dot_general(a, b, (((0,), (0,)), ((), ())), preferred_element_type=F32)


def kernel(
    ids_ref, cnt_ref, q_ref, kv_ref, go_ref, w_ref,
    gq_ref, gm_ref,
    wg, halo, kst, ds, own, gsend, grecv, aall,
    far, relay, near, final, keep,
    zs, zr, xs, xr, hs, hr, xhs, xhr, bs, br, bhs, bhr, bzs, bzr, gs_, gr_, as_, ar_,
    fs, fr, ns, nr, ks, kr,
):
    t = lax.axis_index("tgt")
    y = lax.axis_index("sec")
    core = t % 2
    chip = t // 2
    z = chip % NZ
    x = chip // NZ

    def at(xx, zz, cc, yy):
        return {"tgt": (((xx + NX) % NX) * NZ + (zz + NZ) % NZ) * 2 + cc, "sec": (yy + NY) % NY}

    below = {"tgt": (t + 63) % 64, "sec": y}
    above = {"tgt": (t + 1) % 64, "sec": y}
    partner = {"tgt": t + 1 - 2 * core, "sec": y}
    zto = (at(x, z + 1, core, y), at(x, z - 1, core, y))
    xto = (at(x + 1, z, core, y), at(x - 1, z, core, y))

    barrier = pltpu.get_barrier_semaphore()
    peers = [below, above, *zto, *xto]
    for cc in range(2):
        peers += [at(x, z, cc, y + 1), at(x, z, cc, y - 1)]
    for peer in peers:
        pl.semaphore_signal(barrier, inc=1, device_id=peer, device_id_type=MESH)
    pl.semaphore_wait(barrier, len(peers))

    def remote(src, dst, ssem, rsem, dev):
        return pltpu.make_async_remote_copy(
            src_ref=src, dst_ref=dst, send_sem=ssem, recv_sem=rsem, device_id=dev, device_id_type=MESH
        )

    def zpiece(zz, c0, cn):
        return wg.at[pl.ds(c0, cn), x, zz, pl.ds(0, LEAD), :]

    def zcopy(way, step, half):
        zz = (z - step + NZ) % NZ if way == 0 else (z + step) % NZ
        c0, cn = (way, 1) if half else (0, 2)
        ref = zpiece(zz, c0, cn)
        return remote(ref, ref, zs.at[way, step], zr.at[way, step], zto[way])

    def zarrive(way, step, half):
        zz = (z - step - 1 + NZ) % NZ if way == 0 else (z + step + 1) % NZ
        c0, cn = (way, 1) if half else (0, 2)
        ref = zpiece(zz, c0, cn)
        remote(ref, ref, zs.at[way, step], zr.at[way, step], zto[way]).wait_recv()

    def zof(d):
        return (z + jnp.where(d % 2 == 1, NZ - (d + 1) // 2, d // 2)) % NZ

    def xpiece(xx, d, c0, cn):
        return wg.at[pl.ds(c0, cn), (xx + NX) % NX, zof(d), pl.ds(0, LEAD), :]

    def xcopy(way, d):
        ref = xpiece(x, d, 0, 2)
        return remote(ref, ref, xs.at[way, d], xr.at[way, d], xto[way])

    def xarrive(way, d):
        ref = xpiece(x - 1 + 2 * way, d, 0, 2)
        remote(ref, ref, xs.at[way, d], xr.at[way, d], xto[way]).wait_recv()

    def xhcopy(way, d):
        ref = xpiece(x - 1 + 2 * way, d, way, 1)
        return remote(ref, ref, xhs.at[way, d], xhr.at[way, d], xto[way])

    def xharrive(way, d):
        ref = xpiece(x + 2, d, way, 1)
        remote(ref, ref, xhs.at[way, d], xhr.at[way, d], xto[way]).wait_recv()

    def bpiece(xx, c0, cn):
        return wg.at[pl.ds(c0, cn), (xx + NX) % NX, z, pl.ds(LEAD, 64 - LEAD), :]

    def bcopy(way):
        ref = bpiece(x, 0, 2)
        return remote(ref, ref, bs.at[way], br.at[way], xto[way])

    def barrive(way):
        ref = bpiece(x - 1 + 2 * way, 0, 2)
        remote(ref, ref, bs.at[way], br.at[way], xto[way]).wait_recv()

    def bhcopy(way):
        ref = bpiece(x - 1 + 2 * way, way, 1)
        return remote(ref, ref, bhs.at[way], bhr.at[way], xto[way])

    def bharrive(way):
        ref = bpiece(x + 2, way, 1)
        remote(ref, ref, bhs.at[way], bhr.at[way], xto[way]).wait_recv()

    def bzpiece(zz, c0, cn):
        return wg.at[pl.ds(c0, cn), :, (zz + NZ) % NZ, pl.ds(LEAD, 64 - LEAD), :]

    def bzcopy(way, step):
        c0, cn = (way, 1) if step == 3 else (0, 2)
        ref = bzpiece(z - step if way == 0 else z + step, c0, cn)
        return remote(ref, ref, bzs.at[way, step], bzr.at[way, step], zto[way])

    def bzarrive(way, step):
        c0, cn = (way, 1) if step == 3 else (0, 2)
        ref = bzpiece(z - step - 1 if way == 0 else z + step + 1, c0, cn)
        remote(ref, ref, bzs.at[way, step], bzr.at[way, step], zto[way]).wait_recv()

    def cols(p):
        return pl.ds(pl.multiple_of(p * 128, 128), 128)

    def hcopy(side, p):
        return remote(
            kv_ref.at[:, :, :, cols(p)], halo.at[side, :, :, :, cols(p)],
            hs.at[side, p], hr.at[side, p], above if side else below,
        )

    def gcopy(side, p):
        return remote(
            gsend.at[side, :, :, :, cols(p)], grecv.at[side, :, :, :, cols(p)],
            gs_.at[side, p], gr_.at[side, p], above if side else below,
        )

    def acopy(p):
        ref = aall.at[core, :, :, :, cols(p)]
        return remote(ref, ref, as_.at[p], ar_.at[p], partner)

    def aarrive(p):
        ref = aall.at[1 - core, :, :, :, cols(p)]
        remote(ref, ref, as_.at[p], ar_.at[p], partner).wait_recv()

    def place(c):
        return pltpu.make_async_copy(w_ref.at[c], wg.at[c, x, z], ks.at[c])

    for c in range(2):
        place(c).start()
    for side in range(2):
        hcopy(side, 0).start()
    for c in range(2):
        place(c).wait()
    for way in range(2):
        zcopy(way, 0, False).start()
        bcopy(way).start()
        xcopy(way, 0).start()

    @pl.loop(1, PAIRS)
    def _(p):
        for side in range(2):
            hcopy(side, p).start()

    def step(d):
        @pl.when(d % 2 == 1)
        def _():
            k = (d - 1) // 2

            @pl.when(d < 5)
            def _():
                zarrive(0, k, False)
                zcopy(0, k + 1, False).start()

            @pl.when(d == 5)
            def _():
                zarrive(0, k, False)
                zcopy(0, 3, True).start()

            @pl.when(d == 7)
            def _():
                zarrive(0, 3, True)
                zarrive(1, 3, True)

        @pl.when(d % 2 == 0)
        def _():
            k = d // 2 - 1

            @pl.when(d < 6)
            def _():
                zarrive(1, k, False)
                zcopy(1, k + 1, False).start()

            @pl.when(d == 6)
            def _():
                zarrive(1, k, False)
                zcopy(1, 3, True).start()

        for way in range(2):
            xcopy(way, d).start()

    def forward(d):
        for way in range(2):
            xarrive(way, d)
            xhcopy(way, d).start()

    lane = lax.broadcasted_iota(jnp.int32, (BLOCK, 128), 1)
    low_lane = lane < 64
    sub = lax.broadcasted_iota(jnp.int32, (128, BLOCK), 0)
    low_sub = sub < 64
    ds[:, :, SLOTS] = jnp.zeros((2, 2, BLOCK, 128), F32)
    first = (t - 1) * 2
    zero = jnp.zeros((BLOCK, 128), BF16)

    def attend(p, i):
        rows = pl.ds(i * BLOCK, BLOCK)
        q = q_ref[rows, cols(p)] * jnp.asarray(0.125, BF16)
        g = go_ref[rows, cols(p)]
        q2 = jnp.concatenate([jnp.where(low_lane, q, zero), jnp.where(low_lane, zero, q)], axis=0)
        g2 = jnp.concatenate([jnp.where(low_lane, g, zero), jnp.where(low_lane, zero, g)], axis=0)
        places = [jnp.clip(ids_ref[i, s] - first, 0, EXT - 1) for s in range(SLOTS)]
        k = jnp.concatenate([kst[0, pos] for pos in places], axis=0)
        v = jnp.concatenate([kst[1, pos] for pos in places], axis=0)
        scores = nt(k, q2)
        gprobs = nt(v, g2)
        top = jnp.max(scores, axis=0, keepdims=True)
        expo = []
        for s in range(SLOTS):
            off = jnp.where(s < cnt_ref[i], 0.0, 1e30).astype(F32)
            expo.append(jnp.exp(scores[s * BLOCK:(s + 1) * BLOCK] - (top + off)))
        expo = jnp.concatenate(expo, axis=0)
        probs = expo * (1.0 / jnp.sum(expo, axis=0, keepdims=True))
        half = probs.astype(BF16)
        delta = jnp.sum(half.astype(F32) * gprobs, axis=0, keepdims=True)
        ghalf = (probs * (gprobs - delta)).astype(BF16)
        gk = nn(ghalf, q2)
        gv = nn(half, g2)
        for s in range(SLOTS):
            ds[i, 0, s] = gk[s * BLOCK:(s + 1) * BLOCK]
            ds[i, 1, s] = gv[s * BLOCK:(s + 1) * BLOCK]
        gqt = tn(k, ghalf)
        gqt = jnp.where(low_sub, gqt[:, :BLOCK], gqt[:, BLOCK:])
        gq_ref[rows, cols(p)] = (0.125 * jnp.transpose(gqt)).astype(BF16)

    def slot_of(i, j):
        found = jnp.int32(SLOTS)
        for s in range(SLOTS):
            hit = (ids_ref[i, s] - first == j) & (s < cnt_ref[i])
            found = jnp.where(hit, jnp.int32(s), found)
        return found

    def finish(p):
        for side in range(2):
            gcopy(side, p).wait_recv()
        total = own[:, :, :, cols(p)] + grecv[0, :, :, :, cols(p)].astype(F32)
        total = total + grecv[1, :, :, :, cols(p)].astype(F32)
        aall[core, :, :, :, cols(p)] = total.astype(BF16)
        acopy(p).start()

    @pl.loop(0, PAIRS)
    def _(p):
        @pl.when(p >= 1)
        def _():
            step(p)

        @pl.when(p == 2)
        def _():
            for way in range(2):
                barrive(way)
                bhcopy(way).start()

        @pl.when(p == 4)
        def _():
            for way in range(2):
                bharrive(way)
            for way in range(2):
                bzcopy(way, 0).start()

        for side in range(2):
            hcopy(side, p).wait_recv()
        kst[:, 0:2] = halo[1, :, :, :, cols(p)]
        kst[:, 2:4] = kv_ref[:, :, :, cols(p)]
        kst[:, 4:6] = halo[0, :, :, :, cols(p)]
        for i in range(2):
            attend(p, i)
        for j in range(EXT):
            place0, place1 = slot_of(0, j), slot_of(1, j)
            for c in range(2):
                both = ds[0, c, place0] + ds[1, c, place1]
                if j < 2:
                    gsend[0, c, j, :, cols(p)] = both.astype(BF16)
                elif j < 4:
                    own[c, j - 2, :, cols(p)] = both
                else:
                    gsend[1, c, j - 4, :, cols(p)] = both.astype(BF16)
        for side in range(2):
            gcopy(side, p).start()

        @pl.when(p >= 4)
        def _():
            finish(p - 4)
            forward(p - 4)

    @pl.loop(4, PAIRS)
    def _(p):
        finish(p)

    for step_ in range(1, 4):
        for way in range(2):
            bzarrive(way, step_ - 1)
            bzcopy(way, step_).start()
        forward(3 + step_)
    forward(7)
    for way in range(2):
        bzarrive(way, 3)

    @pl.loop(0, PAIRS)
    def _(d):
        for way in range(2):
            xharrive(way, d)
        aarrive(d)

    def fcopy(way):
        return remote(far.at[way], relay.at[way], fs.at[way], fr.at[way], at(x, z, core, y + 1 - 2 * way))

    def ncopy(way, cc):
        return remote(
            near.at[way, cc], final.at[way, core], ns.at[way, cc], nr.at[way, core],
            at(x, z, cc, y + 1 - 2 * way),
        )

    def narrive(way, k):
        remote(
            near.at[way, 0], final.at[way, k], ns.at[way, 0], nr.at[way, k], at(x, z, core, y + 1 - 2 * way)
        ).wait_recv()

    def kcopy():
        return remote(far.at[0], keep.at[core], ks.at[2], kr.at[0], partner)

    def product(dest, cc):
        total = None
        for c in range(2):
            a = aall[cc, c].reshape(2 * BLOCK, PAIRS * 128)
            w = wg[c, dest].reshape(NZ * 64, PAIRS * 128)
            part = nt(a, w)
            total = part if total is None else total + part
        return total


    for cc in range(2):
        far[cc] = product((y + 2) % NY, cc).astype(BF16)
        fcopy(cc).start()
    for way in range(2):
        dest = (y + 1 - 2 * way + NY) % NY
        near[way, 1 - way] = product(dest, 1 - way).astype(BF16)
        ncopy(way, 1 - way).start()
        total = product(dest, way)
        fcopy(way).wait_recv()
        near[way, way] = (total + relay[way].astype(F32)).astype(BF16)
        ncopy(way, way).start()
    fcopy(0).wait_send()
    fcopy(1).wait_send()
    far[0] = product(y, 1 - core).astype(BF16)
    kcopy().start()
    keep[core] = product(y, core).astype(BF16)
    for way in range(2):
        for k in range(2):
            narrive(way, k)
    remote(far.at[0], keep.at[1 - core], ks.at[2], kr.at[0], partner).wait_recv()
    low = lax.broadcasted_iota(jnp.int32, (2 * BLOCK, 128), 1) < 64
    for q in range(4):
        c = pl.ds(q * 128, 128)
        parts = []
        for k in range(2):
            parts.append(
                final[0, k, :, c].astype(F32) + final[1, k, :, c].astype(F32) + keep[k, :, c].astype(F32)
            )
        a, b = parts
        gm_ref[:, pl.ds(q * 256, 128)] = jnp.where(low, a, pltpu.roll(b, 64, 1)).astype(BF16)
        gm_ref[:, pl.ds(q * 256 + 128, 128)] = jnp.where(low, pltpu.roll(a, 64, 1), b).astype(BF16)

    for way in range(2):
        for k in range(3):
            zcopy(way, k, False).wait_send()
        zcopy(way, 3, True).wait_send()
        bcopy(way).wait_send()
        bhcopy(way).wait_send()
        for k in range(4):
            bzcopy(way, k).wait_send()
        for cc in range(2):
            ncopy(way, cc).wait_send()
    kcopy().wait_send()

    @pl.loop(0, PAIRS)
    def _(p):
        for way in range(2):
            xcopy(way, p).wait_send()
            xhcopy(way, p).wait_send()
            hcopy(way, p).wait_send()
            gcopy(way, p).wait_send()
        acopy(p).wait_send()


def per_device(queries, key_values, grad_out, block_ids, block_count, kv_weight):
    rows, width = queries.shape
    dma = pltpu.SemaphoreType.DMA
    kv = key_values.reshape(2, 2, BLOCK, width)
    vmem = pl.BlockSpec(memory_space=pltpu.VMEM)
    smem = pl.BlockSpec(memory_space=pltpu.SMEM)
    return pl.pallas_call(
        kernel,
        out_shape=(
            jax.ShapeDtypeStruct((rows, width), BF16),
            jax.ShapeDtypeStruct((rows, width), BF16),
        ),
        in_specs=[smem, smem, vmem, vmem, vmem, vmem],
        out_specs=(vmem, vmem),
        scratch_shapes=[
            pltpu.VMEM((2, NX, NZ, 64, width), BF16),
            pltpu.VMEM((2, 2, 2, BLOCK, width), BF16),
            pltpu.VMEM((2, EXT, BLOCK, 128), BF16),
            pltpu.VMEM((2, 2, SLOTS + 1, BLOCK, 128), F32),
            pltpu.VMEM((2, 2, BLOCK, width), F32),
            pltpu.VMEM((2, 2, 2, BLOCK, width), BF16),
            pltpu.VMEM((2, 2, 2, BLOCK, width), BF16),
            pltpu.VMEM((2, 2, 2, BLOCK, width), BF16),
            pltpu.VMEM((2, 2 * BLOCK, 512), BF16),
            pltpu.VMEM((2, 2 * BLOCK, 512), BF16),
            pltpu.VMEM((2, 2, 2 * BLOCK, 512), BF16),
            pltpu.VMEM((2, 2, 2 * BLOCK, 512), BF16),
            pltpu.VMEM((2, 2 * BLOCK, 512), BF16),
            dma((2, 4)), dma((2, 4)),
            dma((2, PAIRS)), dma((2, PAIRS)),
            dma((2, PAIRS)), dma((2, PAIRS)),
            dma((2, PAIRS)), dma((2, PAIRS)),
            dma((2,)), dma((2,)),
            dma((2,)), dma((2,)),
            dma((2, 4)), dma((2, 4)),
            dma((2, PAIRS)), dma((2, PAIRS)),
            dma((PAIRS,)), dma((PAIRS,)),
            dma((2,)), dma((2,)),
            dma((2, 2)), dma((2, 2)),
            dma((3,)), dma((1,)),
        ],
        compiler_params=pltpu.CompilerParams(
            collective_id=0, has_side_effects=True, vmem_limit_bytes=56 * 1024 * 1024
        ),
    )(block_ids, block_count, queries, kv, grad_out, kv_weight)


def solution(mesh):
    return jax.shard_map(
        per_device,
        mesh=mesh,
        in_specs=(
            P("tgt", "sec"),
            P(None, "tgt", "sec"),
            P("tgt", "sec"),
            P("tgt", None),
            P("tgt"),
            P(None, "tgt", "sec"),
        ),
        out_specs=(P("tgt", "sec"), P("tgt", "sec")),
        check_vma=False,
    )
```

time: 271 us -> 117 us (0.43)
  Pallas kernels: 0 us -> 114 us
  waiting for transfers between devices: 99.2 us -> 0 us
  matrix products: 64.3 us -> 0 us
  local copies, waits for them, and re-layouts: 67 us -> 2.72 us
  between operations: 14.1 us -> 0.65 us
  starting transfers between devices: 12.5 us -> 0 us
  other arithmetic: 12.4 us -> 0 us
    pallas_call x0 -> x1, Pallas kernels: none -> 114 us  [per_device(): pl.pallas_call(kernel, out_shape=(jax.ShapeDtypeStruct((rows, width), BF1...]
    psum x1 -> x0, waiting for transfers between devices: 73.1 us -> none  [per_device(): lax.psum(partial_memory.astype(jnp.bfloat16), 'sec').astype(jnp.float32)]
    dot_general x13 -> x0, matrix products: 57.6 us -> none  [the longest x2 26.7 us: block_step(): jnp.einsum('sj,csrx->cjrx', targets, pair_grads, precision=lax.Precision....]
    another operation x8 -> x0, local copies, waits for them, and re-layouts: 27.6 us -> none  [block_step(): jnp.stack([grad_key, grad_value]).reshape(2, SLOTS, BLOCK, width_here)]
    ppermute x4 -> x0, waiting for transfers between devices: 25.4 us -> none  [the longest x2 11.7 us: from_behind(): return lax.ppermute(block, axis, route)]
    ppermute x4 -> x0, starting transfers between devices: 12.4 us -> none  [the longest x2 5.56 us: from_behind(): return lax.ppermute(block, axis, route)]
    while x41 -> x0, local copies, waits for them, and re-layouts: 11.6 us -> none  [the longest x1 7.02 us: per_device(): spread_blocks, query_blocks = lax.scan(block_step, start, inputs)]
    slice x7 -> x0, local copies, waits for them, and re-layouts: 8.97 us -> none  [the longest x4 7.31 us: block_step(): value_rows = picked[1].reshape(SLOTS * BLOCK, heads_here, HEAD_DIM)]
  transfers between devices with their start and end apart: 6 -> 0, of which waited for: 5 -> 0; matrix products, arithmetic and copies ran while one was open for 45% -> 0% of each run, Pallas kernels for 0% -> 0%
where the time goes in v1:
time: 117 us
  Pallas kernels  114 us (97%)
  local copies, waits for them, and re-layouts  2.72 us (2%)
    pallas_call x1, Pallas kernels, per_device(): pl.pallas_call(kernel, out_shape=(jax.ShapeDtypeStruct((rows, width), BF1...  114 us
    unnamed x4, local copies, waits for them, and re-layouts  2.72 us

profile of v1, /device:TPU:1, one launch (start us, length us, event | category | flops | bytes accessed | tf_op | source)
XLA Modules:
  0.0 117.2 jit_solution(6553783310173674989)
XLA Ops:
  0.6 113.9 %shard_map.77 = (bf16[256,1024]{1,0:T(8,128)(2,1)}, bf16[256,1024]{1,0:T(8,128)(2,1)}) custom-call(s32[2,4]{1,0:T(2,128)} %ids_ref.1, s32[2]{0:T(128)} %cnt_ref.1, bf16[256,1024]{1,0:T(8,128)(2,1)} %q_ref.1, bf16[2,2,128,1024]{3,2,1,0:T(8,128)(2,1)} %bitcast.1, bf16[256,1024]{1,0:T(8,128)(2,1)} %go_ref.1, bf16[2,64,1024]{2,1,0:T(8,128)(2,1)} %w_ref.1), custom_call_target="tpu_custom_call" | custom-call | tf_op jit(solution)/shard_map/pallas_call | solution.py:426
  114.5 0.0 copy-start
  114.5 1.9 %copy.10 = bf16[256,1024]{1,0:T(8,128)(2,1)} copy(bf16[256,1024]{1,0:T(8,128)(2,1)} %get-tuple-element.4) | data formatting | bytes 1048576
  116.4 0.0 copy-done
  116.4 0.8 copy.11
Async XLA Ops:
  114.5 1.9 %copy-start = (bf16[256,1024]{1,0:T(8,128)(2,1)S(1)}, bf16[256,1024]{1,0:T(8,128)(2,1)}, u32[]{:S(2)}) copy-start(bf16[256,1024]{1,0:T(8,128)(2,1)} %get-tuple-element.5) | copy-start | bytes 1572868

commit v2 on v1

--- a/solution.py
+++ b/solution.py
@@ -14,6 +14,7 @@
 PAIRS = 8
 NX, NZ, NY = 4, 8, 4
 LEAD = 48
+MOVED = 5
 F32 = jnp.float32
 BF16 = jnp.bfloat16
 
@@ -33,10 +34,11 @@
 def kernel(
     ids_ref, cnt_ref, q_ref, kv_ref, go_ref, w_ref,
     gq_ref, gm_ref,
-    wg, halo, kst, ds, own, gsend, grecv, aall,
-    far, relay, near, final, keep,
-    zs, zr, xs, xr, hs, hr, xhs, xhr, bs, br, bhs, bhr, bzs, bzr, gs_, gr_, as_, ar_,
-    fs, fr, ns, nr, ks, kr,
+    wga, wgb, halo, kst, ds, own, gsend, grecv, aall, cur, pend,
+    far_a, relay_a, near_a, final_a, cross_a, keep_a,
+    far_b, relay_b, near_b, final_b, cross_b, keep_b,
+    zs, zr, xs, xr, hs, hr, xhs, xhr, bs, br, bhs, bhr, bzs, bzr, gs_, gr_, as_, ar_, ps,
+    fs, fr, ns, nr, ks, kr, fbs, fbr, nbs, nbr, kbs, kbr,
 ):
     t = lax.axis_index("tgt")
     y = lax.axis_index("sec")
@@ -68,7 +70,7 @@
         )
 
     def zpiece(zz, c0, cn):
-        return wg.at[pl.ds(c0, cn), x, zz, pl.ds(0, LEAD), :]
+        return wga.at[pl.ds(c0, cn), x, zz]
 
     def zcopy(way, step, half):
         zz = (z - step + NZ) % NZ if way == 0 else (z + step) % NZ
@@ -86,7 +88,7 @@
         return (z + jnp.where(d % 2 == 1, NZ - (d + 1) // 2, d // 2)) % NZ
 
     def xpiece(xx, d, c0, cn):
-        return wg.at[pl.ds(c0, cn), (xx + NX) % NX, zof(d), pl.ds(0, LEAD), :]
+        return wga.at[pl.ds(c0, cn), (xx + NX) % NX, zof(d)]
 
     def xcopy(way, d):
         ref = xpiece(x, d, 0, 2)
@@ -96,16 +98,30 @@
         ref = xpiece(x - 1 + 2 * way, d, 0, 2)
         remote(ref, ref, xs.at[way, d], xr.at[way, d], xto[way]).wait_recv()
 
-    def xhcopy(way, d):
-        ref = xpiece(x - 1 + 2 * way, d, way, 1)
+    def xhcopy(way, d, whole):
+        ref = xpiece(x - 1 + 2 * way, d, 0 if whole else way, 2 if whole else 1)
         return remote(ref, ref, xhs.at[way, d], xhr.at[way, d], xto[way])
 
-    def xharrive(way, d):
-        ref = xpiece(x + 2, d, way, 1)
+    def halves(d, act):
+        moved = d < MOVED
+        for way in range(2):
+            whole = moved & (z == (NZ - 1 if way == 0 else 0))
+            none = moved & (z == (0 if way == 0 else NZ - 1))
+
+            @pl.when(whole)
+            def _():
+                act(way, d, True)
+
+            @pl.when(jnp.logical_not(whole | none))
+            def _():
+                act(way, d, False)
+
+    def xharrive(way, d, whole):
+        ref = xpiece(x + 2, d, 0 if whole else way, 2 if whole else 1)
         remote(ref, ref, xhs.at[way, d], xhr.at[way, d], xto[way]).wait_recv()
 
     def bpiece(xx, c0, cn):
-        return wg.at[pl.ds(c0, cn), (xx + NX) % NX, z, pl.ds(LEAD, 64 - LEAD), :]
+        return wgb.at[pl.ds(c0, cn), (xx + NX) % NX, z]
 
     def bcopy(way):
         ref = bpiece(x, 0, 2)
@@ -123,18 +139,23 @@
         ref = bpiece(x + 2, way, 1)
         remote(ref, ref, bhs.at[way], bhr.at[way], xto[way]).wait_recv()
 
-    def bzpiece(zz, c0, cn):
-        return wg.at[pl.ds(c0, cn), :, (zz + NZ) % NZ, pl.ds(LEAD, 64 - LEAD), :]
-
-    def bzcopy(way, step):
-        c0, cn = (way, 1) if step == 3 else (0, 2)
-        ref = bzpiece(z - step if way == 0 else z + step, c0, cn)
-        return remote(ref, ref, bzs.at[way, step], bzr.at[way, step], zto[way])
-
-    def bzarrive(way, step):
-        c0, cn = (way, 1) if step == 3 else (0, 2)
-        ref = bzpiece(z - step - 1 if way == 0 else z + step + 1, c0, cn)
-        remote(ref, ref, bzs.at[way, step], bzr.at[way, step], zto[way]).wait_recv()
+    def bzpiece(zz, c):
+        return wgb.at[c, :, (zz + NZ) % NZ]
+
+    def bzcopy(way, step, c):
+        ref = bzpiece(z - step if way == 0 else z + step, c)
+        return remote(ref, ref, bzs.at[way, step, c], bzr.at[way, step, c], zto[way])
+
+    def bzarrive(way, step, c):
+        ref = bzpiece(z - step - 1 if way == 0 else z + step + 1, c)
+        remote(ref, ref, bzs.at[way, step, c], bzr.at[way, step, c], zto[way]).wait_recv()
+
+    def bzforward(step):
+        for c in range(2):
+            for way in range(2):
+                bzarrive(way, step - 1, c)
+                if step < 3 or c == way:
+                    bzcopy(way, step, c).start()
 
     def cols(p):
         return pl.ds(pl.multiple_of(p * 128, 128), 128)
@@ -152,28 +173,32 @@
         )
 
     def acopy(p):
-        ref = aall.at[core, :, :, :, cols(p)]
+        ref = aall.at[core, :, cols(p), :]
         return remote(ref, ref, as_.at[p], ar_.at[p], partner)
 
     def aarrive(p):
-        ref = aall.at[1 - core, :, :, :, cols(p)]
+        ref = aall.at[1 - core, :, cols(p), :]
         remote(ref, ref, as_.at[p], ar_.at[p], partner).wait_recv()
 
-    def place(c):
-        return pltpu.make_async_copy(w_ref.at[c], wg.at[c, x, z], ks.at[c])
+    def place(c, lead):
+        if lead:
+            return pltpu.make_async_copy(w_ref.at[c, pl.ds(0, LEAD)], wga.at[c, x, z], ps.at[c, 0])
+        return pltpu.make_async_copy(w_ref.at[c, pl.ds(LEAD, 64 - LEAD)], wgb.at[c, x, z], ps.at[c, 1])
 
     for c in range(2):
-        place(c).start()
+        place(c, True).start()
+        place(c, False).start()
     for side in range(2):
         hcopy(side, 0).start()
     for c in range(2):
-        place(c).wait()
+        place(c, True).wait()
+        place(c, False).wait()
     for way in range(2):
+        bcopy(way).start()
         zcopy(way, 0, False).start()
-        bcopy(way).start()
         xcopy(way, 0).start()
 
-    @pl.loop(1, PAIRS)
+    @pl.loop(1, 4)
     def _(p):
         for side in range(2):
             hcopy(side, p).start()
@@ -218,7 +243,7 @@
     def forward(d):
         for way in range(2):
             xarrive(way, d)
-            xhcopy(way, d).start()
+        halves(d, lambda *a: xhcopy(*a).start())
 
     lane = lax.broadcasted_iota(jnp.int32, (BLOCK, 128), 1)
     low_lane = lane < 64
@@ -270,27 +295,37 @@
             gcopy(side, p).wait_recv()
         total = own[:, :, :, cols(p)] + grecv[0, :, :, :, cols(p)].astype(F32)
         total = total + grecv[1, :, :, :, cols(p)].astype(F32)
-        aall[core, :, :, :, cols(p)] = total.astype(BF16)
+        for c in range(2):
+            aall[core, c, cols(p), :] = jnp.transpose(total[c].reshape(2 * BLOCK, 128)).astype(BF16)
         acopy(p).start()
 
     @pl.loop(0, PAIRS)
     def _(p):
-        @pl.when(p >= 1)
-        def _():
-            step(p)
-
-        @pl.when(p == 2)
+        @pl.when(p == 1)
         def _():
             for way in range(2):
                 barrive(way)
                 bhcopy(way).start()
 
-        @pl.when(p == 4)
+        @pl.when((p == 2) | (p == 5))
+        def _():
+            d = jnp.where(p == 2, 1, 3)
+            step(d)
+            step(d + 1)
+
+        @pl.when(p == 2)
+        def _():
+            for late in range(4, PAIRS):
+                for side in range(2):
+                    hcopy(side, late).start()
+
+        @pl.when(p == 6)
         def _():
             for way in range(2):
                 bharrive(way)
-            for way in range(2):
-                bzcopy(way, 0).start()
+            for c in range(2):
+                for way in range(2):
+                    bzcopy(way, 0, c).start()
 
         for side in range(2):
             hcopy(side, p).wait_recv()
@@ -312,88 +347,192 @@
         for side in range(2):
             gcopy(side, p).start()
 
-        @pl.when(p >= 4)
-        def _():
-            finish(p - 4)
-            forward(p - 4)
+    step(5)
+    step(6)
+
+    @pl.loop(0, 3)
+    def _(d):
+        forward(d)
+
+    step(7)
+    forward(3)
+    forward(4)
+
+    @pl.loop(0, 4)
+    def _(p):
+        finish(p)
+
+    bzforward(1)
+    forward(5)
+    forward(6)
 
     @pl.loop(4, PAIRS)
     def _(p):
         finish(p)
 
-    for step_ in range(1, 4):
-        for way in range(2):
-            bzarrive(way, step_ - 1)
-            bzcopy(way, step_).start()
-        forward(3 + step_)
     forward(7)
-    for way in range(2):
-        bzarrive(way, 3)
+    bzforward(2)
 
     @pl.loop(0, PAIRS)
     def _(d):
-        for way in range(2):
-            xharrive(way, d)
         aarrive(d)
 
-    def fcopy(way):
-        return remote(far.at[way], relay.at[way], fs.at[way], fr.at[way], at(x, z, core, y + 1 - 2 * way))
-
-    def ncopy(way, cc):
-        return remote(
-            near.at[way, cc], final.at[way, core], ns.at[way, cc], nr.at[way, core],
-            at(x, z, cc, y + 1 - 2 * way),
-        )
-
-    def narrive(way, k):
-        remote(
-            near.at[way, 0], final.at[way, k], ns.at[way, 0], nr.at[way, k], at(x, z, core, y + 1 - 2 * way)
-        ).wait_recv()
-
-    def kcopy():
-        return remote(far.at[0], keep.at[core], ks.at[2], kr.at[0], partner)
-
-    def product(dest, cc):
-        total = None
-        for c in range(2):
-            a = aall[cc, c].reshape(2 * BLOCK, PAIRS * 128)
-            w = wg[c, dest].reshape(NZ * 64, PAIRS * 128)
-            part = nt(a, w)
-            total = part if total is None else total + part
-        return total
-
-
-    for cc in range(2):
-        far[cc] = product((y + 2) % NY, cc).astype(BF16)
-        fcopy(cc).start()
+    def side_of(way):
+        return y + 1 - 2 * way
+
+    def sums(n, work, halfs, sem, slot):
+        far, relay, near, final, cross, keep = halfs
+        fs, fr, ns, nr, ks, kr = sem
+
+        def fcopy(way):
+            return remote(work(far, way), work(relay, way), fs(way), fr(way), at(x, z, core, side_of(way)))
+
+        def ncopy(way, cc):
+            return remote(
+                work(near, way, cc), work(final, way, core), ns(way, cc), nr(way, core),
+                at(x, z, cc, side_of(way)),
+            )
+
+        def narrive(way, k):
+            remote(
+                work(near, way, 0), work(final, way, k), ns(way, 0), nr(way, k), at(x, z, core, side_of(way))
+            ).wait_recv()
+
+        def kcopy():
+            return remote(work(cross), work(keep, core), ks(), kr(), partner)
+
+        def karrive():
+            remote(work(cross), work(keep, 1 - core), ks(), kr(), partner).wait_recv()
+
+        def put(ref, values):
+            ref[...] = values.reshape(ref.shape).astype(BF16)
+
+        def begin(rel):
+            mine = cur.at[pl.ds(0, n)]
+
+            @pl.when(rel == 2)
+            def _():
+                for cc in range(2):
+                    put(work(far, cc), mine[:, cc * 256:(cc + 1) * 256])
+                    fcopy(cc).start()
+
+            for way in range(2):
+                @pl.when(rel == 1 + 2 * way)
+                def _():
+                    cc = 1 - way
+                    put(work(near, way, cc), mine[:, cc * 256:(cc + 1) * 256])
+                    ncopy(way, cc).start()
+                    pend[slot(way), pl.ds(0, n)] = mine[:, way * 256:(way + 1) * 256]
+
+            @pl.when(rel == 0)
+            def _():
+                other = pl.ds(pl.multiple_of((1 - core) * 256, 256), 256)
+                here = pl.ds(pl.multiple_of(core * 256, 256), 256)
+                put(work(cross), mine[:, other])
+                kcopy().start()
+                put(work(keep, core), mine[:, here])
+
+        def complete(rel):
+            for way in range(2):
+                @pl.when(rel == 1 + 2 * way)
+                def _():
+                    fcopy(way).wait_recv()
+                    came = work(relay, way)[...].astype(F32).reshape(n, 256)
+                    put(work(near, way, way), pend[slot(way), pl.ds(0, n)] + came)
+                    ncopy(way, way).start()
+
+        def arrive():
+            for way in range(2):
+                for k in range(2):
+                    narrive(way, k)
+            karrive()
+
+        def leave():
+            for way in range(2):
+                fcopy(way).wait_send()
+                for cc in range(2):
+                    ncopy(way, cc).wait_send()
+            kcopy().wait_send()
+
+        return begin, complete, arrive, leave
+
+    def part_a(u):
+        def work(ref, *lead):
+            return ref.at[(*lead, pl.ds(2 * u, 2))]
+
+        return sums(2 * LEAD, work, (far_a, relay_a, near_a, final_a, cross_a, keep_a), (
+            lambda w: fs.at[w, u], lambda w: fr.at[w, u], lambda w, c: ns.at[w, c, u], lambda w, k: nr.at[w, k, u],
+            lambda: ks.at[u], lambda: kr.at[u],
+        ), lambda way: u)
+
+    def work_b(ref, *lead):
+        return ref.at[lead] if lead else ref
+
+    part_b = sums(NZ * (64 - LEAD), work_b, (far_b, relay_b, near_b, final_b, cross_b, keep_b), (
+        lambda w: fbs.at[w], lambda w: fbr.at[w], lambda w, c: nbs.at[w, c], lambda w, k: nbr.at[w, k],
+        lambda: kbs.at[0], lambda: kbr.at[0],
+    ), lambda way: 4 + way)
+
+    def product(rows):
+        weights = [rows(c) for c in range(2)]
+        for cc in range(2):
+            total = nn(weights[0], aall[cc, 0]) + nn(weights[1], aall[cc, 1])
+            cur[pl.ds(0, total.shape[0]), pl.ds(cc * 256, 256)] = total
+
+    def dest_a(i):
+        e = i // 4
+        return (x + jnp.where(e == 1, 1, jnp.where(e == 2, 3, jnp.where(e == 3, 2, 0)))) % NX
+
+    @pl.loop(0, 16)
+    def _(i):
+        u = i % 4
+        dest = dest_a(i)
+
+        @pl.when(i >= 12)
+        def _():
+            halves(2 * u, xharrive)
+            halves(2 * u + 1, xharrive)
+
+        product(lambda c: jnp.concatenate([wga[c, dest, zof(2 * u)], wga[c, dest, zof(2 * u + 1)]], axis=0))
+
+        @pl.when(i >= 4)
+        def _():
+            part_a(u)[1]((dest_a(i - 4) - y + NY) % NY)
+
+        part_a(u)[0]((dest - y + NY) % NY)
+
+        @pl.when(i == 5)
+        def _():
+            bzforward(3)
+
     for way in range(2):
-        dest = (y + 1 - 2 * way + NY) % NY
-        near[way, 1 - way] = product(dest, 1 - way).astype(BF16)
-        ncopy(way, 1 - way).start()
-        total = product(dest, way)
-        fcopy(way).wait_recv()
-        near[way, way] = (total + relay[way].astype(F32)).astype(BF16)
-        ncopy(way, way).start()
-    fcopy(0).wait_send()
-    fcopy(1).wait_send()
-    far[0] = product(y, 1 - core).astype(BF16)
-    kcopy().start()
-    keep[core] = product(y, core).astype(BF16)
-    for way in range(2):
+        bzarrive(way, 3, way)
+    for rel in (2, 1, 3, 0):
+        dest = (y + rel) % NY
+        product(lambda c: wgb[c, dest].reshape(NZ * (64 - LEAD), PAIRS * 128))
+        part_b[0](jnp.int32(rel))
+
+    @pl.loop(0, 4)
+    def _(u):
+        part_a(u)[1]((dest_a(15) - y + NY) % NY)
+
+    for rel in (1, 3):
+        part_b[1](jnp.int32(rel))
+    for u in range(4):
+        part_a(u)[2]()
+    part_b[2]()
+
+    @pl.loop(0, NZ)
+    def _(d):
+        zz = zof(d)
+        rows = []
         for k in range(2):
-            narrive(way, k)
-    remote(far.at[0], keep.at[1 - core], ks.at[2], kr.at[0], partner).wait_recv()
-    low = lax.broadcasted_iota(jnp.int32, (2 * BLOCK, 128), 1) < 64
-    for q in range(4):
-        c = pl.ds(q * 128, 128)
-        parts = []
-        for k in range(2):
-            parts.append(
-                final[0, k, :, c].astype(F32) + final[1, k, :, c].astype(F32) + keep[k, :, c].astype(F32)
-            )
-        a, b = parts
-        gm_ref[:, pl.ds(q * 256, 128)] = jnp.where(low, a, pltpu.roll(b, 64, 1)).astype(BF16)
-        gm_ref[:, pl.ds(q * 256 + 128, 128)] = jnp.where(low, pltpu.roll(a, 64, 1), b).astype(BF16)
+            for final, keep, at_ in ((final_a, keep_a, d), (final_b, keep_b, zz)):
+                rows.append(
+                    final[0, k, at_].astype(F32) + final[1, k, at_].astype(F32) + keep[k, at_].astype(F32)
+                )
+        block = jnp.concatenate(rows, axis=0)
+        gm_ref[:, cols(zz)] = jnp.transpose(block).astype(BF16)
 
     for way in range(2):
         for k in range(3):
@@ -402,18 +541,20 @@
         bcopy(way).wait_send()
         bhcopy(way).wait_send()
         for k in range(4):
-            bzcopy(way, k).wait_send()
-        for cc in range(2):
-            ncopy(way, cc).wait_send()
-    kcopy().wait_send()
+            for c in range(2):
+                if k < 3 or c == way:
+                    bzcopy(way, k, c).wait_send()
+    for u in range(4):
+        part_a(u)[3]()
+    part_b[3]()
 
     @pl.loop(0, PAIRS)
     def _(p):
         for way in range(2):
             xcopy(way, p).wait_send()
-            xhcopy(way, p).wait_send()
             hcopy(way, p).wait_send()
             gcopy(way, p).wait_send()
+        halves(p, lambda *a: xhcopy(*a).wait_send())
         acopy(p).wait_send()
 
 
@@ -432,31 +573,35 @@
         in_specs=[smem, smem, vmem, vmem, vmem, vmem],
         out_specs=(vmem, vmem),
         scratch_shapes=[
-            pltpu.VMEM((2, NX, NZ, 64, width), BF16),
+            pltpu.VMEM((2, NX, NZ, LEAD, width), BF16),
+            pltpu.VMEM((2, NX, NZ, 64 - LEAD, width), BF16),
             pltpu.VMEM((2, 2, 2, BLOCK, width), BF16),
             pltpu.VMEM((2, EXT, BLOCK, 128), BF16),
             pltpu.VMEM((2, 2, SLOTS + 1, BLOCK, 128), F32),
             pltpu.VMEM((2, 2, BLOCK, width), F32),
             pltpu.VMEM((2, 2, 2, BLOCK, width), BF16),
             pltpu.VMEM((2, 2, 2, BLOCK, width), BF16),
-            pltpu.VMEM((2, 2, 2, BLOCK, width), BF16),
-            pltpu.VMEM((2, 2 * BLOCK, 512), BF16),
-            pltpu.VMEM((2, 2 * BLOCK, 512), BF16),
-            pltpu.VMEM((2, 2, 2 * BLOCK, 512), BF16),
-            pltpu.VMEM((2, 2, 2 * BLOCK, 512), BF16),
-            pltpu.VMEM((2, 2 * BLOCK, 512), BF16),
+            pltpu.VMEM((2, 2, width, 2 * BLOCK), BF16),
+            pltpu.VMEM((NZ * (64 - LEAD), 4 * BLOCK), F32),
+            pltpu.VMEM((6, NZ * (64 - LEAD), 2 * BLOCK), F32),
+            *[pltpu.VMEM((*lead, NZ, n, 2 * BLOCK), BF16)
+              for n in (LEAD, 64 - LEAD) for lead in ((2,), (2,), (2, 2), (2, 2), (), (2,))],
             dma((2, 4)), dma((2, 4)),
             dma((2, PAIRS)), dma((2, PAIRS)),
             dma((2, PAIRS)), dma((2, PAIRS)),
             dma((2, PAIRS)), dma((2, PAIRS)),
             dma((2,)), dma((2,)),
             dma((2,)), dma((2,)),
-            dma((2, 4)), dma((2, 4)),
+            dma((2, 4, 2)), dma((2, 4, 2)),
             dma((2, PAIRS)), dma((2, PAIRS)),
             dma((PAIRS,)), dma((PAIRS,)),
+            dma((2, 2)),
+            dma((2, 4)), dma((2, 4)),
+            dma((2, 2, 4)), dma((2, 2, 4)),
+            dma((4,)), dma((4,)),
             dma((2,)), dma((2,)),
             dma((2, 2)), dma((2, 2)),
-            dma((3,)), dma((1,)),
+            dma((1,)), dma((1,)),
         ],
         compiler_params=pltpu.CompilerParams(
             collective_id=0, has_side_effects=True, vmem_limit_bytes=56 * 1024 * 1024

time: 117 us -> 112 us (0.957); the launches traced: 117 us -> 110 us
  Pallas kernels: 114 us -> 107 us
    pallas_call x1, Pallas kernels: 114 us -> 107 us  [per_device(): pl.pallas_call(kernel, out_shape=(jax.ShapeDtypeStruct((rows, width), BF1...]
where the time goes in v2:
time: 112 us; the launch traced here: 110 us
  Pallas kernels  107 us (96%)
  local copies, waits for them, and re-layouts  2.72 us (2%)
    pallas_call x1, Pallas kernels, per_device(): pl.pallas_call(kernel, out_shape=(jax.ShapeDtypeStruct((rows, width), BF1...  107 us
    unnamed x4, local copies, waits for them, and re-layouts  2.72 us

profile of v2, /device:TPU:1, one launch (start us, length us, event | category | flops | bytes accessed | tf_op | source)
XLA Modules:
  0.0 110.2 jit_solution(5587697474172543069)
XLA Ops:
  0.6 106.8 %shard_map.77 = (bf16[256,1024]{1,0:T(8,128)(2,1)}, bf16[256,1024]{1,0:T(8,128)(2,1)}) custom-call(s32[2,4]{1,0:T(2,128)} %ids_ref.1, s32[2]{0:T(128)} %cnt_ref.1, bf16[256,1024]{1,0:T(8,128)(2,1)} %q_ref.1, bf16[2,2,128,1024]{3,2,1,0:T(8,128)(2,1)} %bitcast.1, bf16[256,1024]{1,0:T(8,128)(2,1)} %go_ref.1, bf16[2,64,1024]{2,1,0:T(8,128)(2,1)} %w_ref.1), custom_call_target="tpu_custom_call" | custom-call | tf_op jit(solution)/shard_map/pallas_call | solution.py:567
  107.4 0.0 copy-start
  107.4 1.9 %copy.10 = bf16[256,1024]{1,0:T(8,128)(2,1)} copy(bf16[256,1024]{1,0:T(8,128)(2,1)} %get-tuple-element.4) | data formatting | bytes 1048576
  109.4 0.0 copy-done
  109.4 0.8 copy.11
Async XLA Ops:
  107.4 1.9 %copy-start = (bf16[256,1024]{1,0:T(8,128)(2,1)S(1)}, bf16[256,1024]{1,0:T(8,128)(2,1)}, u32[]{:S(2)}) copy-start(bf16[256,1024]{1,0:T(8,128)(2,1)} %get-tuple-element.5) | copy-start | bytes 1572868

commit v3 on v2

--- a/solution.py
+++ b/solution.py
@@ -14,7 +14,8 @@
 PAIRS = 8
 NX, NZ, NY = 4, 8, 4
 LEAD = 48
-MOVED = 5
+MOVED = 6
+S34 = 5
 F32 = jnp.float32
 BF16 = jnp.bfloat16
 
@@ -94,6 +95,9 @@
         ref = xpiece(x, d, 0, 2)
         return remote(ref, ref, xs.at[way, d], xr.at[way, d], xto[way])
 
+    def hot(way):
+        return z == (0 if way == 0 else NZ - 1)
+
     def xarrive(way, d):
         ref = xpiece(x - 1 + 2 * way, d, 0, 2)
         remote(ref, ref, xs.at[way, d], xr.at[way, d], xto[way]).wait_recv()
@@ -102,11 +106,11 @@
         ref = xpiece(x - 1 + 2 * way, d, 0 if whole else way, 2 if whole else 1)
         return remote(ref, ref, xhs.at[way, d], xhr.at[way, d], xto[way])
 
-    def halves(d, act):
+    def halves(d, act, ways=(0, 1)):
         moved = d < MOVED
-        for way in range(2):
-            whole = moved & (z == (NZ - 1 if way == 0 else 0))
-            none = moved & (z == (0 if way == 0 else NZ - 1))
+        for way in ways:
+            whole = moved & hot(1 - way)
+            none = moved & hot(way)
 
             @pl.when(whole)
             def _():
@@ -198,7 +202,7 @@
         zcopy(way, 0, False).start()
         xcopy(way, 0).start()
 
-    @pl.loop(1, 4)
+    @pl.loop(1, 6)
     def _(p):
         for side in range(2):
             hcopy(side, p).start()
@@ -240,10 +244,22 @@
         for way in range(2):
             xcopy(way, d).start()
 
+    def send_half(*which):
+        xhcopy(*which).start()
+
     def forward(d):
         for way in range(2):
-            xarrive(way, d)
-        halves(d, lambda *a: xhcopy(*a).start())
+            @pl.when(jnp.logical_not(hot(way)))
+            def _():
+                xarrive(way, d)
+                halves(d, send_half, (way,))
+
+    def forward_late(d):
+        for way in range(2):
+            @pl.when(hot(way))
+            def _():
+                xarrive(way, d)
+                halves(d, send_half, (way,))
 
     lane = lax.broadcasted_iota(jnp.int32, (BLOCK, 128), 1)
     low_lane = lane < 64
@@ -307,7 +323,7 @@
                 barrive(way)
                 bhcopy(way).start()
 
-        @pl.when((p == 2) | (p == 5))
+        @pl.when((p == 2) | (p == S34))
         def _():
             d = jnp.where(p == 2, 1, 3)
             step(d)
@@ -315,7 +331,7 @@
 
         @pl.when(p == 2)
         def _():
-            for late in range(4, PAIRS):
+            for late in range(6, PAIRS):
                 for side in range(2):
                     hcopy(side, late).start()
 
@@ -323,9 +339,6 @@
         def _():
             for way in range(2):
                 bharrive(way)
-            for c in range(2):
-                for way in range(2):
-                    bzcopy(way, 0, c).start()
 
         for side in range(2):
             hcopy(side, p).wait_recv()
@@ -344,34 +357,30 @@
                     own[c, j - 2, :, cols(p)] = both
                 else:
                     gsend[1, c, j - 4, :, cols(p)] = both.astype(BF16)
+    step(5)
+    step(6)
+
+    @pl.loop(0, PAIRS)
+    def _(p):
         for side in range(2):
             gcopy(side, p).start()
 
-    step(5)
-    step(6)
-
-    @pl.loop(0, 3)
+    step(7)
+    for c in range(2):
+        for way in range(2):
+            bzcopy(way, 0, c).start()
+
+    @pl.loop(0, 6)
     def _(d):
         forward(d)
 
-    step(7)
-    forward(3)
-    forward(4)
-
-    @pl.loop(0, 4)
+    @pl.loop(0, PAIRS)
     def _(p):
         finish(p)
 
     bzforward(1)
-    forward(5)
     forward(6)
-
-    @pl.loop(4, PAIRS)
-    def _(p):
-        finish(p)
-
     forward(7)
-    bzforward(2)
 
     @pl.loop(0, PAIRS)
     def _(d):
@@ -488,6 +497,12 @@
         u = i % 4
         dest = dest_a(i)
 
+        @pl.when(i == 4)
+        def _():
+            @pl.loop(0, PAIRS)
+            def _(d):
+                forward_late(d)
+
         @pl.when(i >= 12)
         def _():
             halves(2 * u, xharrive)
@@ -501,9 +516,10 @@
 
         part_a(u)[0]((dest - y + NY) % NY)
 
-        @pl.when(i == 5)
-        def _():
-            bzforward(3)
+        for step_ in (2, 3):
+            @pl.when(i == (7 if step_ == 2 else 14))
+            def _():
+                bzforward(step_)
 
     for way in range(2):
         bzarrive(way, 3, way)

time: 112 us -> 105 us (0.938); the launches traced: 110 us -> 105 us
  Pallas kernels: 107 us -> 102 us
    pallas_call x1, Pallas kernels: 107 us -> 102 us  [per_device(): pl.pallas_call(kernel, out_shape=(jax.ShapeDtypeStruct((rows, width), BF1...]
where the time goes in v3:
time: 105 us
  Pallas kernels  102 us (97%)
  local copies, waits for them, and re-layouts  2.72 us (3%)
    pallas_call x1, Pallas kernels, per_device(): pl.pallas_call(kernel, out_shape=(jax.ShapeDtypeStruct((rows, width), BF1...  102 us
    unnamed x4, local copies, waits for them, and re-layouts  2.72 us

profile of v3, /device:TPU:1, one launch (start us, length us, event | category | flops | bytes accessed | tf_op | source)
XLA Modules:
  0.0 104.9 jit_solution(6340511297538578222)
XLA Ops:
  0.6 101.6 %shard_map.77 = (bf16[256,1024]{1,0:T(8,128)(2,1)}, bf16[256,1024]{1,0:T(8,128)(2,1)}) custom-call(s32[2,4]{1,0:T(2,128)} %ids_ref.1, s32[2]{0:T(128)} %cnt_ref.1, bf16[256,1024]{1,0:T(8,128)(2,1)} %q_ref.1, bf16[2,2,128,1024]{3,2,1,0:T(8,128)(2,1)} %bitcast.1, bf16[256,1024]{1,0:T(8,128)(2,1)} %go_ref.1, bf16[2,64,1024]{2,1,0:T(8,128)(2,1)} %w_ref.1), custom_call_target="tpu_custom_call" | custom-call | tf_op jit(solution)/shard_map/pallas_call | solution.py:583
  102.2 0.0 copy-start
  102.2 1.9 %copy.10 = bf16[256,1024]{1,0:T(8,128)(2,1)} copy(bf16[256,1024]{1,0:T(8,128)(2,1)} %get-tuple-element.4) | data formatting | bytes 1048576
  104.1 0.0 copy-done
  104.1 0.8 copy.11
Async XLA Ops:
  102.2 1.9 %copy-start = (bf16[256,1024]{1,0:T(8,128)(2,1)S(1)}, bf16[256,1024]{1,0:T(8,128)(2,1)}, u32[]{:S(2)}) copy-start(bf16[256,1024]{1,0:T(8,128)(2,1)} %get-tuple-element.5) | copy-start | bytes 1572868

commit v4 on v3

--- a/solution.py
+++ b/solution.py
@@ -490,14 +490,16 @@
 
     def dest_a(i):
         e = i // 4
-        return (x + jnp.where(e == 1, 1, jnp.where(e == 2, 3, jnp.where(e == 3, 2, 0)))) % NX
+        swap = z == NZ - 1
+        one, two = jnp.where(swap, 3, 1), jnp.where(swap, 1, 3)
+        return (x + jnp.where(e == 1, one, jnp.where(e == 2, two, jnp.where(e == 3, 2, 0)))) % NX
 
     @pl.loop(0, 16)
     def _(i):
         u = i % 4
         dest = dest_a(i)
 
-        @pl.when(i == 4)
+        @pl.when(i == 8)
         def _():
             @pl.loop(0, PAIRS)
             def _(d):

time: 105 us -> 102 us (0.971)
  Pallas kernels: 102 us -> 98 us
    pallas_call x1, Pallas kernels: 102 us -> 98 us  [per_device(): pl.pallas_call(kernel, out_shape=(jax.ShapeDtypeStruct((rows, width), BF1...]
where the time goes in v4:
time: 102 us; the launch traced here: 101 us
  Pallas kernels  98 us (96%)
  local copies, waits for them, and re-layouts  2.72 us (3%)
    pallas_call x1, Pallas kernels, per_device(): pl.pallas_call(kernel, out_shape=(jax.ShapeDtypeStruct((rows, width), BF1...  98 us
    unnamed x4, local copies, waits for them, and re-layouts  2.72 us

profile of v4, /device:TPU:1, one launch (start us, length us, event | category | flops | bytes accessed | tf_op | source)
XLA Modules:
  0.0 101.4 jit_solution(9474572501744044657)
XLA Ops:
  0.6 98.0 %shard_map.77 = (bf16[256,1024]{1,0:T(8,128)(2,1)}, bf16[256,1024]{1,0:T(8,128)(2,1)}) custom-call(s32[2,4]{1,0:T(2,128)} %ids_ref.1, s32[2]{0:T(128)} %cnt_ref.1, bf16[256,1024]{1,0:T(8,128)(2,1)} %q_ref.1, bf16[2,2,128,1024]{3,2,1,0:T(8,128)(2,1)} %bitcast.1, bf16[256,1024]{1,0:T(8,128)(2,1)} %go_ref.1, bf16[2,64,1024]{2,1,0:T(8,128)(2,1)} %w_ref.1), custom_call_target="tpu_custom_call" | custom-call | tf_op jit(solution)/shard_map/pallas_call | solution.py:585
  98.7 0.0 copy-start
  98.7 1.9 %copy.10 = bf16[256,1024]{1,0:T(8,128)(2,1)} copy(bf16[256,1024]{1,0:T(8,128)(2,1)} %get-tuple-element.4) | data formatting | bytes 1048576
  100.6 0.0 copy-done
  100.6 0.8 copy.11
Async XLA Ops:
  98.7 1.9 %copy-start = (bf16[256,1024]{1,0:T(8,128)(2,1)S(1)}, bf16[256,1024]{1,0:T(8,128)(2,1)}, u32[]{:S(2)}) copy-start(bf16[256,1024]{1,0:T(8,128)(2,1)} %get-tuple-element.5) | copy-start | bytes 1572868
